TPU v7x, 32 devices: a whole 2x2x4 slice. The times are simulated.
32 devices in a mesh: src: 4 (over y, core), rcv: 8 (over z, x).
Axes of the slice: x: 2, y: 2, z: 4, core: 2. Of those that a mesh axis runs over, the one named last changes fastest.
Arguments:
- data: bfloat16 [2, 4096, 4096], P(None, ('src', 'rcv')), may hold values from -0.8984375 to 0.8984375
- fill_mask: int32 [4096, 4096], P(('src', 'rcv')), may hold values 0 or 1
- obliquity: float32 [4096], replicated, may hold values from 0.25 to 4
- aperture: int32 [8, 8, 8], P('src'), may hold values from 0 to 7, as said below
- lengths: int32 [8, 8], P('src', 'rcv'), may hold values from 1 to 8, as said below
Outputs:
- predicted: float32 [2, 4096, 4096], P(None, 'src', 'rcv')
Inputs may be any that keep to these rules, and one draw needn't show every extreme that they name: `aperture`: every entry is a tile index; the 8 entries of one output tile are distinct; only the first lengths entries of a list are used. `lengths`: some output tile uses all 8 entries of its list.
All inputs are finite; a program needn't handle non-finite values. No bound on the sum of `fill_mask` on one device may be relied on, other than what follows from the above.
Results may differ from a plain program's by a relative error of at most 0.0028.
Values may be sent and summed in bfloat16 or wider, within the bound.
No kernel may reach another device: no remote copies, remote signals or barrier semaphores. Data moves between devices by JAX's collectives and lax.ppermute only.
A program may use at most 128 MiB of HBM per device.

v0:
```python
import jax
import jax.numpy as jnp
from jax import lax
from jax.sharding import PartitionSpec as P

TILE_SIZE = 512


def complex_product(left_pair, right_pair):
    left_wide = jnp.concatenate([left_pair[0], left_pair[1]], axis=1)
    upper = jnp.concatenate([right_pair[0], right_pair[1]], axis=1)
    lower = jnp.concatenate([-right_pair[1], right_pair[0]], axis=1)
    right_wide = jnp.concatenate([upper, lower], axis=0)
    return jnp.dot(left_wide, right_wide, preferred_element_type=jnp.float32)


def predict_tile(tile_row, my_lists, slot_count, left_piece, column_data):

    def add_slot(slot_index, summed):
        inner_tile = my_lists[tile_row, slot_index]
        left_pair = left_piece(tile_row, slot_index, inner_tile)
        right_pair = lax.dynamic_slice(
            column_data, (0, inner_tile * TILE_SIZE, 0), (2, TILE_SIZE, TILE_SIZE)
        )
        return summed + complex_product(left_pair, right_pair)

    initial = jnp.zeros((TILE_SIZE, 2 * TILE_SIZE), jnp.float32)
    return -lax.fori_loop(0, slot_count, add_slot, initial)


def local(data, fill_mask, obliquity, aperture, lengths):
    local_rows = data.shape[1]
    station_total = data.shape[2]
    src_count = lax.axis_size("src")
    rcv_count = lax.axis_size("rcv")
    devices = src_count * rcv_count
    blocks = data.reshape(2, 1, local_rows, devices, local_rows)
    arrived = lax.all_to_all(blocks, ("src", "rcv"), split_axis=3, concat_axis=1, tiled=True)
    arrived = arrived.reshape(2, devices, local_rows, local_rows)
    transposed = jnp.transpose(arrived, (0, 3, 1, 2)).reshape(2, local_rows, station_total)
    filled = jnp.where(fill_mask[None] == 1, data, transposed)
    tile_block = lax.all_to_all(filled, "rcv", split_axis=2, concat_axis=1, tiled=True)
    span = tile_block.shape[1]
    gains = lax.dynamic_slice_in_dim(obliquity, lax.axis_index("src") * span, span)
    weighted = (tile_block.astype(jnp.float32) * gains[None, :, None]).astype(jnp.bfloat16)
    column_data = lax.all_gather(weighted, "src", axis=1, tiled=True)
    rcv_index = lax.axis_index("rcv")
    my_lists = lax.dynamic_index_in_dim(aperture, rcv_index, 1, keepdims=False)
    tile_rows = span // TILE_SIZE
    row_data = lax.all_gather(tile_block, "rcv", axis=2, tiled=True)

    def left_piece(tile_row, slot_index, inner_tile):
        return lax.dynamic_slice(
            row_data, (0, tile_row * TILE_SIZE, inner_tile * TILE_SIZE), (2, TILE_SIZE, TILE_SIZE)
        )

    results = []
    for tile_row in range(tile_rows):
        results.append(
            predict_tile(tile_row, my_lists, lengths[tile_row, 0], left_piece, column_data)
        )
    stacked = jnp.stack(results).reshape(tile_rows, TILE_SIZE, 2, TILE_SIZE)
    return jnp.transpose(stacked, (2, 0, 1, 3)).reshape(2, tile_rows * TILE_SIZE, TILE_SIZE)


def solution(mesh):
    placed = (
        P(None, ("src", "rcv"), None),
        P(("src", "rcv"), None),
        P(),
        P("src", None, None),
        P("src", "rcv"),
    )
    return jax.shard_map(
        local, mesh=mesh, in_specs=placed, out_specs=P(None, "src", "rcv"), check_vma=False
    )
```

profile of v0, /device:TPU:6, one launch (start us, length us, event | category | flops | bytes accessed | tf_op | source)
XLA Modules:
  0.0 575.6 jit_solution(8887815864550951217)
XLA Ops:
  6.5 3.1 copy.19
  11.1 6.1 %all-to-all-start = ((bf16[2,1,128,32,128]{2,4,0,1,3:T(8,128)(2,1)}), bf16[2,1,128,32,128]{2,4,0,1,3:T(8,128)(2,1)}, u32[]{:S(2)}, u32[]{:S(2)}) async-start(bf16[2,1,128,32,128]{2,4,0,1,3:T(8,128)(2,1)} %copy.17), calls=%async_computation | async-start | bytes 4194304 | tf_op jit(solution)/shard_map/all_to_all | solution.py:38
  17.3 1.9 broadcast_compare_fusion
  20.2 45.0 %all-to-all-done = bf16[2,1,128,32,128]{2,4,0,1,3:T(8,128)(2,1)} async-done(((bf16[2,1,128,32,128]{2,4,0,1,3:T(8,128)(2,1)}), bf16[2,1,128,32,128]{2,4,0,1,3:T(8,128)(2,1)}, u32[]{:S(2)}, u32[]{:S(2)}) %all-to-all-start) | async-done | bytes 2097184 | tf_op jit(solution)/shard_map/all_to_all | solution.py:38
  65.1 4.1 copy.18
  69.2 2.1 broadcast_select_fusion
  71.3 18.1 %copy.20 = bf16[2,128,4096]{1,0,2:T(2,128)(2,1)} copy(bf16[2,128,4096]{1,2,0:T(8,128)(2,1)S(1)} %broadcast_select_fusion) | data formatting | bytes 4194304 | tf_op jit(solution)/shard_map/jit(_where)/select_n | solution.py:41
  89.5 5.3 all-to-all-start.1
  94.8 48.2 %all-to-all-done.1 = bf16[2,128,4096]{1,0,2:T(2,128)(2,1)S(1)} async-done(((bf16[2,128,4096]{1,0,2:T(2,128)(2,1)}), bf16[2,128,4096]{1,0,2:T(2,128)(2,1)S(1)}, u32[]{:S(2)}, u32[]{:S(2)}) %all-to-all-start.1) | async-done | bytes 2097184 | tf_op jit(solution)/shard_map/all_to_all | solution.py:42
  144.3 4.7 copy.21
  149.1 2.1 multiply_convert_fusion
  152.6 55.1 %all-gather.5.cloned.1.call-done = bf16[2,4096,512]{2,1,0:T(8,128)(2,1)} async-done(((bf16[2,1024,512]{2,1,0:T(8,128)(2,1)}), bf16[2,4096,512]{2,1,0:T(8,128)(2,1)}) %all-gather.5.cloned.1.call-update) | async-done | bytes 8388624 | tf_op jit(solution)/shard_map/all_gather | solution.py:46
  207.7 230.3 %all-gather.3.cloned.1.call-done = bf16[2,1024,4096]{2,1,0:T(8,128)(2,1)} async-done(((bf16[2,1024,512]{2,1,0:T(8,128)(2,1)}), bf16[2,1024,4096]{2,1,0:T(8,128)(2,1)}) %all-gather.3.cloned.1.call-update) | async-done | bytes 16777232 | tf_op jit(solution)/shard_map/all_gather | solution.py:50
  438.2 58.5 %while.21 = (s32[]{:T(128)}, f32[512,1024]{1,0:T(8,128)S(1)}, s32[]{:T(128)}, s32[2,8]{1,0:T(2,128)S(1)}, bf16[2,1024,4096]{2,1,0:T(8,128)(2,1)}, /*index=5*/bf1...) while((s32[]{:T(128)}, f32[512,1024]{1,0:T(8,128)S(1)}, ...), condition=%wide.region_3.4_spmd, body=%wide.region_2.3_spmd.sunk | while | flops 1085538304 | bytes 11534561 | solution.py:28
  442.7 1.5 dynamic-slice_bitcast_fusion.13
  449.9 1.5 dynamic-slice_bitcast_fusion.13
  457.1 1.5 dynamic-slice_bitcast_fusion.13
  464.4 1.5 dynamic-slice_bitcast_fusion.13
  471.6 1.5 dynamic-slice_bitcast_fusion.13
  478.8 1.5 dynamic-slice_bitcast_fusion.13
  486.0 1.5 dynamic-slice_bitcast_fusion.13
  493.3 1.5 dynamic-slice_bitcast_fusion.13
  496.8 1.5 neg.13
  498.3 3.0 stack.10
  501.3 1.7 copy.23
  503.3 56.9 %while.20 = (s32[]{:T(128)}, f32[512,1024]{1,0:T(8,128)S(1)}, s32[]{:T(128)}, s32[2,8]{1,0:T(2,128)S(1)}, bf16[2,1024,4096]{2,1,0:T(8,128)(2,1)}, /*index=5*/bf1...) while((s32[]{:T(128)}, f32[512,1024]{1,0:T(8,128)S(1)}, ...), condition=%wide.region_1.2_spmd, body=%wide.region_0.1_spmd.sunk | while | flops 1085538304 | bytes 11534561 | solution.py:28
  507.5 1.5 dynamic-slice_bitcast_fusion.12
  514.5 1.5 dynamic-slice_bitcast_fusion.12
  521.6 1.5 dynamic-slice_bitcast_fusion.12
  560.2 1.5 neg.12
  561.7 3.0 stack.9
  566.3 2.5 pad_maximum_fusion
  (78 shorter events, 64.1 us)
Async XLA Ops:
  6.5 145.4 %copy-start = (s32[2,8,8]{2,1,0:T(8,128)S(1)}, s32[2,8,8]{2,1,0:T(8,128)}, u32[]{:S(2)}) copy-start(s32[2,8,8]{2,1,0:T(8,128)} %param.12) | copy-start | bytes 1540
  11.1 54.0 %all-to-all-start = ((bf16[2,1,128,32,128]{2,4,0,1,3:T(8,128)(2,1)}), bf16[2,1,128,32,128]{2,4,0,1,3:T(8,128)(2,1)}, u32[]{:S(2)}, u32[]{:S(2)}) async-start(bf16[2,1,128,32,128]{2,4,0,1,3:T(8,128)(2,1)} %copy.17), calls=%async_computation | async-start | bytes 4194304 | tf_op jit(solution)/shard_map/all_to_all | solution.py:38
  89.5 53.5 %all-to-all-start.1 = ((bf16[2,128,4096]{1,0,2:T(2,128)(2,1)}), bf16[2,128,4096]{1,0,2:T(2,128)(2,1)S(1)}, u32[]{:S(2)}, u32[]{:S(2)}) async-start(bf16[2,128,4096]{1,0,2:T(2,128)(2,1)} %copy.20), calls=%async_computation.1 | async-start | bytes 4194304 | tf_op jit(solution)/shard_map/all_to_all | solution.py:42
  94.8 112.9 %all-gather.5.cloned.1.call-start = ((), (), s32[]{:S(2)}) async-start(), calls=%async_computation.3 | async-start | bytes 10485760 | tf_op jit(solution)/shard_map/all_gather | solution.py:46
  143.0 1.3 copy-start.3
  144.3 4.7 dynamic-slice-start
  149.1 2.1 copy-start.2
  151.1 0.8 copy-start.5
  151.2 286.8 %all-gather.3.cloned.1.call-start = ((), (), s32[]{:S(2)}) async-start(), calls=%async_computation.2 | async-start | bytes 18874368 | tf_op jit(solution)/shard_map/all_gather | solution.py:50
  564.8 1.6 copy-start.4
  566.3 2.5 copy-start.1
Sparse Core Ops, SparseCore 0:
  151.3 56.3 all-gather.4
  209.7 228.1 all-gather.2
where the time goes:
time: 578 us; the launch traced here: 576 us
  waiting for transfers between devices  379 us (66%)
  local copies, waits for them, and re-layouts  67.9 us (12%)
  loops' own time  42.4 us (7%)
  other arithmetic  39.8 us (7%)
  matrix products  21.2 us (4%)
  between operations  13.6 us (2%)
  starting transfers between devices  11.5 us (2%)
    all_gather x1, waiting for transfers between devices, local(): row_data = lax.all_gather(tile_block, 'rcv', axis=2, tiled=True)  230 us
    all_gather x1, waiting for transfers between devices, local(): column_data = lax.all_gather(weighted, 'src', axis=1, tiled=True)  55.1 us
    all_to_all x1, waiting for transfers between devices, local(): lax.all_to_all(filled, 'rcv', split_axis=2, concat_axis=1, tiled=True)  48.2 us
    all_to_all x1, waiting for transfers between devices, local(): lax.all_to_all(blocks, ('src', 'rcv'), split_axis=3, concat_axis=1, tiled...  45 us
    another operation x2, loops' own time, predict_tile(): return -lax.fori_loop(0, slot_count, add_slot, initial)  42.4 us
    squeeze x16, local copies, waits for them, and re-layouts, complex_product(): left_wide = jnp.concatenate([left_pair[0], left_pair[1]], axis=1)  23.7 us
    dot_general x16, matrix products, complex_product(): return jnp.dot(left_wide, right_wide, preferred_element_type=jnp.float32)  21.2 us
    neg x16, other arithmetic, complex_product(): lower = jnp.concatenate([-right_pair[1], right_pair[0]], axis=1)  18.7 us
  transfers between devices with their start and end apart: 4, of which 4 were waited for; matrix products, arithmetic and copies ran while one was open for 1% of the time, Pallas kernels for 0%

commit v1 on v0

--- a/solution.py
+++ b/solution.py
@@ -39,7 +39,19 @@
     arrived = arrived.reshape(2, devices, local_rows, local_rows)
     transposed = jnp.transpose(arrived, (0, 3, 1, 2)).reshape(2, local_rows, station_total)
     filled = jnp.where(fill_mask[None] == 1, data, transposed)
-    tile_block = lax.all_to_all(filled, "rcv", split_axis=2, concat_axis=1, tiled=True)
+    ways, here = (lax.axis_size("rcv"), lax.axis_index("rcv"))
+    width = filled.shape[2] // ways
+    shape = list(filled.shape)
+    shape[2] = width
+    height = shape[1]
+    shape[1] = height * ways
+    full = jnp.zeros(shape, filled.dtype)
+    for mask in range(ways):
+        part = lax.dynamic_slice_in_dim(filled, (here ^ mask) * width, width, axis=2)
+        if mask:
+            part = lax.ppermute(part, "rcv", [(d, d ^ mask) for d in range(ways)])
+        full = lax.dynamic_update_slice_in_dim(full, part, (here ^ mask) * height, axis=1)
+    tile_block = full
     span = tile_block.shape[1]
     gains = lax.dynamic_slice_in_dim(obliquity, lax.axis_index("src") * span, span)
     weighted = (tile_block.astype(jnp.float32) * gains[None, :, None]).astype(jnp.bfloat16)

time: 578 us -> 555 us (0.960)
  local copies, waits for them, and re-layouts: 67.9 us -> 52.8 us
  waiting for transfers between devices: 379 us -> 367 us
    all_to_all x1 -> x0, waiting for transfers between devices: 48.2 us -> none  [local(): lax.all_to_all(filled, 'rcv', split_axis=2, concat_axis=1, tiled=True)]
    ppermute x0 -> x7, waiting for transfers between devices: none -> 28.5 us  [local(): part = lax.ppermute(part, 'rcv', [(d, d ^ mask) for d in range(ways)])]
    select_n x1 -> x0, local copies, waits for them, and re-layouts: 18.1 us -> none  [local(): filled = jnp.where(fill_mask[None] == 1, data, transposed)]
    ppermute x0 -> x7, starting transfers between devices: none -> 9.76 us  [local(): part = lax.ppermute(part, 'rcv', [(d, d ^ mask) for d in range(ways)])]
    all_gather x1, waiting for transfers between devices: 55.1 us -> 62.7 us  [local(): column_data = lax.all_gather(weighted, 'src', axis=1, tiled=True)]
    ppermute x0 -> x7, local copies, waits for them, and re-layouts: none -> 7.6 us  [local(): part = lax.ppermute(part, 'rcv', [(d, d ^ mask) for d in range(ways)])]
  transfers between devices with their start and end apart: 4 -> 10, of which waited for: 4 -> 7; matrix products, arithmetic and copies ran while one was open for 1% -> 2% of each run, Pallas kernels for 0% -> 0%
where the time goes in v1:
time: 555 us; the launch traced here: 553 us
  waiting for transfers between devices  367 us (66%)
  local copies, waits for them, and re-layouts  52.8 us (10%)
  loops' own time  42.5 us (8%)
  other arithmetic  39.6 us (7%)
  matrix products  21.3 us (4%)
  starting transfers between devices  16 us (3%)
  between operations  13.8 us (2%)
    all_gather x1, waiting for transfers between devices, local(): row_data = lax.all_gather(tile_block, 'rcv', axis=2, tiled=True)  230 us
    all_gather x1, waiting for transfers between devices, local(): column_data = lax.all_gather(weighted, 'src', axis=1, tiled=True)  62.7 us
    all_to_all x1, waiting for transfers between devices, local(): lax.all_to_all(blocks, ('src', 'rcv'), split_axis=3, concat_axis=1, tiled...  44.9 us
    another operation x2, loops' own time, predict_tile(): return -lax.fori_loop(0, slot_count, add_slot, initial)  42.5 us
    ppermute x7, waiting for transfers between devices, local(): part = lax.ppermute(part, 'rcv', [(d, d ^ mask) for d in range(ways)])  28.5 us
    squeeze x16, local copies, waits for them, and re-layouts, complex_product(): left_wide = jnp.concatenate([left_pair[0], left_pair[1]], axis=1)  23.6 us
    dot_general x16, matrix products, complex_product(): return jnp.dot(left_wide, right_wide, preferred_element_type=jnp.float32)  21.3 us
    neg x16, other arithmetic, complex_product(): lower = jnp.concatenate([-right_pair[1], right_pair[0]], axis=1)  18.7 us
  transfers between devices with their start and end apart: 10, of which 7 were waited for; matrix products, arithmetic and copies ran while one was open for 2% of the time, Pallas kernels for 0%

profile of v1, /device:TPU:6, one launch (start us, length us, event | category | flops | bytes accessed | tf_op | source)
XLA Modules:
  0.0 552.9 jit_solution(13758410001757228288)
XLA Ops:
  6.5 3.1 copy.15
  11.1 6.1 %all-to-all-start = ((bf16[2,1,128,32,128]{2,4,0,1,3:T(8,128)(2,1)}), bf16[2,1,128,32,128]{2,4,0,1,3:T(8,128)(2,1)}, u32[]{:S(2)}, u32[]{:S(2)}) async-start(bf16[2,1,128,32,128]{2,4,0,1,3:T(8,128)(2,1)} %copy.13), calls=%async_computation | async-start | bytes 4194304 | tf_op jit(solution)/shard_map/all_to_all | solution.py:38
  17.4 1.9 broadcast_compare_fusion
  20.3 44.9 %all-to-all-done = bf16[2,1,128,32,128]{2,4,0,1,3:T(8,128)(2,1)} async-done(((bf16[2,1,128,32,128]{2,4,0,1,3:T(8,128)(2,1)}), bf16[2,1,128,32,128]{2,4,0,1,3:T(8,128)(2,1)}, u32[]{:S(2)}, u32[]{:S(2)}) %all-to-all-start) | async-done | bytes 2097184 | tf_op jit(solution)/shard_map/all_to_all | solution.py:38
  65.1 4.1 copy.14
  69.2 2.1 broadcast_select_fusion
  73.9 2.1 collective-permute-start.2
  77.3 2.6 collective-permute-start.4
  81.2 2.0 collective-permute-start.5
  84.3 7.8 %collective-permute-done.1 = bf16[2,128,512]{1,2,0:T(8,128)(2,1)} collective-permute-done((bf16[2,128,512]{1,2,0:T(8,128)(2,1)S(1)}, bf16[2,128,512]{1,2,0:T(8,128)(2,1)}, u32[]{:S(2)}, u32[]{:S(2)}) %collective-permute-start.1) | collective-permute-done | bytes 262176 | tf_op jit(solution)/shard_map/ppermute | solution.py:52
  93.6 2.0 collective-permute-done.2
  97.9 17.5 %collective-permute-done.4 = bf16[2,128,512]{1,2,0:T(8,128)(2,1)} collective-permute-done((bf16[2,128,512]{1,2,0:T(8,128)(2,1)S(1)}, bf16[2,128,512]{1,2,0:T(8,128)(2,1)}, u32[]{:S(2)}, u32[]{:S(2)}) %collective-permute-start.4) | collective-permute-done | bytes 262176 | tf_op jit(solution)/shard_map/ppermute | solution.py:52
  118.8 2.0 multiply_convert_fusion
  122.2 62.7 %all-gather.5.cloned.1.call-done = bf16[2,4096,512]{2,1,0:T(8,128)(2,1)} async-done(((bf16[2,1024,512]{2,1,0:T(8,128)(2,1)}), bf16[2,4096,512]{2,1,0:T(8,128)(2,1)}) %all-gather.5.cloned.1.call-update) | async-done | bytes 8388624 | tf_op jit(solution)/shard_map/all_gather | solution.py:58
  185.0 230.3 %all-gather.3.cloned.1.call-done = bf16[2,1024,4096]{2,1,0:T(8,128)(2,1)} async-done(((bf16[2,1024,512]{2,1,0:T(8,128)(2,1)}), bf16[2,1024,4096]{2,1,0:T(8,128)(2,1)}) %all-gather.3.cloned.1.call-update) | async-done | bytes 16777232 | tf_op jit(solution)/shard_map/all_gather | solution.py:62
  415.5 58.0 %while.20 = (s32[]{:T(128)}, f32[512,1024]{1,0:T(8,128)S(1)}, s32[]{:T(128)}, s32[2,8]{1,0:T(2,128)S(1)}, bf16[2,1024,4096]{2,1,0:T(8,128)(2,1)}, /*index=5*/bf1...) while((s32[]{:T(128)}, f32[512,1024]{1,0:T(8,128)S(1)}, ...), condition=%wide.region_1.2_spmd, body=%wide.region_0.1_spmd.sunk | while | flops 1085538304 | bytes 11534553 | solution.py:28
  454.6 1.5 dynamic-slice_bitcast_fusion.12
  473.6 1.5 neg.12
  475.0 3.0 stack.9
  478.1 1.8 copy.24
  480.1 57.4 %while.21 = (s32[]{:T(128)}, f32[512,1024]{1,0:T(8,128)S(1)}, s32[]{:T(128)}, s32[2,8]{1,0:T(2,128)S(1)}, bf16[2,1024,4096]{2,1,0:T(8,128)(2,1)}, /*index=5*/bf1...) while((s32[]{:T(128)}, f32[512,1024]{1,0:T(8,128)S(1)}, ...), condition=%wide.region_3.4_spmd, body=%wide.region_2.3_spmd.sunk | while | flops 1085538304 | bytes 11534553 | solution.py:28
  483.2 1.5 dynamic-slice_bitcast_fusion.13
  490.3 1.5 dynamic-slice_bitcast_fusion.13
  497.4 1.5 dynamic-slice_bitcast_fusion.13
  504.5 1.5 dynamic-slice_bitcast_fusion.13
  511.6 1.5 dynamic-slice_bitcast_fusion.13
  518.7 1.5 dynamic-slice_bitcast_fusion.13
  525.8 1.5 dynamic-slice_bitcast_fusion.13
  533.0 1.5 dynamic-slice_bitcast_fusion.13
  537.5 1.5 neg.13
  539.0 3.0 stack.10
  543.6 2.5 pad_maximum_fusion
  (104 shorter events, 78.9 us)
Async XLA Ops:
  6.5 115.1 %copy-start = (s32[2,8,8]{2,1,0:T(8,128)S(1)}, s32[2,8,8]{2,1,0:T(8,128)}, u32[]{:S(2)}) copy-start(s32[2,8,8]{2,1,0:T(8,128)} %param.12) | copy-start | bytes 1540
  11.1 54.0 %all-to-all-start = ((bf16[2,1,128,32,128]{2,4,0,1,3:T(8,128)(2,1)}), bf16[2,1,128,32,128]{2,4,0,1,3:T(8,128)(2,1)}, u32[]{:S(2)}, u32[]{:S(2)}) async-start(bf16[2,1,128,32,128]{2,4,0,1,3:T(8,128)(2,1)} %copy.13), calls=%async_computation | async-start | bytes 4194304 | tf_op jit(solution)/shard_map/all_to_all | solution.py:38
  17.3 167.7 %all-gather.5.cloned.1.call-start = ((), (), s32[]{:S(2)}) async-start(), calls=%async_computation.2 | async-start | bytes 10485760 | tf_op jit(solution)/shard_map/all_gather | solution.py:58
  72.3 8.9 %collective-permute-start = (bf16[2,128,512]{1,2,0:T(8,128)(2,1)}, bf16[2,128,512]{1,2,0:T(8,128)(2,1)}, u32[]{:S(2)}, u32[]{:S(2)}) collective-permute-start(bf16[2,128,512]{1,2,0:T(8,128)(2,1)} %get-tuple-element.113), channel_id=1, source_target_pairs={{0,1},{1,0},{2,3},{3,2},{4,5},{5,4},{6,7},{7,6},{8,9},{9,8},{10,11... | collective-permute-start | bytes 786440 | tf_op jit(solution)/shard_map/ppermute | solution.py:52
  73.8 18.3 %collective-permute-start.1 = (bf16[2,128,512]{1,2,0:T(8,128)(2,1)S(1)}, bf16[2,128,512]{1,2,0:T(8,128)(2,1)}, u32[]{:S(2)}, u32[]{:S(2)}) collective-permute-start(bf16[2,128,512]{1,2,0:T(8,128)(2,1)S(1)} %get-tuple-element.112), channel_id=1, source_target_pairs={{0,2},{1,3},{2,0},{3,1},{4,6},{5,7},{6,4},{7,5},{8,10},{9,11},{10,... | collective-permute-start | bytes 786440 | tf_op jit(solution)/shard_map/ppermute | solution.py:52
  73.9 21.7 %collective-permute-start.2 = (bf16[2,128,512]{1,2,0:T(8,128)(2,1)}, bf16[2,128,512]{1,2,0:T(8,128)(2,1)}, u32[]{:S(2)}, u32[]{:S(2)}) collective-permute-start(bf16[2,128,512]{1,2,0:T(8,128)(2,1)} %get-tuple-element.111), channel_id=1, source_target_pairs={{0,3},{1,2},{2,1},{3,0},{4,7},{5,6},{6,5},{7,4},{8,11},{9,10},{10,... | collective-permute-start | bytes 786440 | tf_op jit(solution)/shard_map/ppermute | solution.py:52
  76.0 20.7 %collective-permute-start.3 = (bf16[2,128,512]{1,2,0:T(8,128)(2,1)}, bf16[2,128,512]{1,2,0:T(8,128)(2,1)}, u32[]{:S(2)}, u32[]{:S(2)}) collective-permute-start(bf16[2,128,512]{1,2,0:T(8,128)(2,1)} %get-tuple-element.110), channel_id=1, source_target_pairs={{0,4},{1,5},{2,6},{3,7},{4,0},{5,1},{6,2},{7,3},{8,12},{9,13},{10,... | collective-permute-start | bytes 786440 | tf_op jit(solution)/shard_map/ppermute | solution.py:52
  77.3 38.1 %collective-permute-start.4 = (bf16[2,128,512]{1,2,0:T(8,128)(2,1)S(1)}, bf16[2,128,512]{1,2,0:T(8,128)(2,1)}, u32[]{:S(2)}, u32[]{:S(2)}) collective-permute-start(bf16[2,128,512]{1,2,0:T(8,128)(2,1)S(1)} %get-tuple-element.109), channel_id=1, source_target_pairs={{0,5},{1,4},{2,7},{3,6},{4,1},{5,0},{6,3},{7,2},{8,13},{9,12},{10,... | collective-permute-start | bytes 786440 | tf_op jit(solution)/shard_map/ppermute | solution.py:52
  81.2 35.3 %collective-permute-start.5 = (bf16[2,128,512]{1,2,0:T(8,128)(2,1)S(1)}, bf16[2,128,512]{1,2,0:T(8,128)(2,1)}, u32[]{:S(2)}, u32[]{:S(2)}) collective-permute-start(bf16[2,128,512]{1,2,0:T(8,128)(2,1)S(1)} %get-tuple-element.108), channel_id=1, source_target_pairs={{0,6},{1,7},{2,4},{3,5},{4,2},{5,3},{6,0},{7,1},{8,14},{9,15},{10,... | collective-permute-start | bytes 786440 | tf_op jit(solution)/shard_map/ppermute | solution.py:52
  92.1 25.6 %collective-permute-start.6 = (bf16[2,128,512]{1,2,0:T(8,128)(2,1)S(1)}, bf16[2,128,512]{1,2,0:T(8,128)(2,1)}, u32[]{:S(2)}, u32[]{:S(2)}) collective-permute-start(bf16[2,128,512]{1,2,0:T(8,128)(2,1)S(1)} %get-tuple-element.107), channel_id=1, source_target_pairs={{0,7},{1,6},{2,5},{3,4},{4,3},{5,2},{6,1},{7,0},{8,15},{9,14},{10,... | collective-permute-start | bytes 786440 | tf_op jit(solution)/shard_map/ppermute | solution.py:52
  97.8 21.0 %dynamic-slice-start = ((f32[4096]{0:T(1024)}, s32[]{:T(128)}), f32[1024]{0:T(1024)S(1)}, s32[]{:S(2)}) async-start(f32[4096]{0:T(1024)} %param.11, s32[]{:T(128)} %select_n.91), calls=%async_computation.3 | async-start | bytes 8704 | tf_op jit(solution)/shard_map/dynamic_slice | solution.py:56
  118.8 2.1 copy-start.2
  120.9 0.8 copy-start.4
  120.9 294.4 %all-gather.3.cloned.1.call-start = ((), (), s32[]{:S(2)}) async-start(), calls=%async_computation.1 | async-start | bytes 18874368 | tf_op jit(solution)/shard_map/all_gather | solution.py:62
  542.1 1.6 copy-start.3
  543.6 2.5 copy-start.1
Sparse Core Ops, SparseCore 0:
  121.0 63.9 all-gather.4
  187.0 228.1 all-gather.2
